TPU v7x, 32 devices: a whole 2x2x4 slice. The times are simulated.
32 devices in a mesh: group: 2 (over y), dp: 4 (over x, core), seq: 4 (over z).
Axes of the slice: x: 2, y: 2, z: 4, core: 2. Of those that a mesh axis runs over, the one named last changes fastest.
Arguments:
- tokens: bfloat16 [8, 1024, 4096], P(('group', 'dp'), 'seq'), parts along dimension 0, may hold values from -6 to 6
- norm_gain: bfloat16 [4096], replicated, may hold values from 0.099609375 to 1.8984375
- qkv_weight: bfloat16 [4096, 3072], P('dp'), may hold values from -4 to 4, as said below
- doc_ids: int32 [8, 1024], P(('group', 'dp'), 'seq'), parts along dimension 0, may hold values from 0 to 5, never falling along the last dimension, each value on 1 to 512 neighbouring positions
Outputs:
- attended: bfloat16 [8, 1024, 2048], P(('group', 'dp'), 'seq'), parts along dimension 0
There are 2 independent parts, one for each index of `group`. A program takes and returns all parts, laid end to end along the dimension named above; an argument that names none is the same for every part. Nothing has to cross between parts.
Inputs may be any that keep to these rules, and one draw needn't show every extreme that they name: `qkv_weight`: in the hidden draw query heads lie close to multiples of their key head. `doc_ids`: ids never fall along a sequence; a document holds at most 512 positions.
All inputs are finite; a program needn't handle non-finite values.
Results may differ from a plain program's by a relative error of at most 0.0075.
Values may be sent and summed in bfloat16 or wider, within the bound.
No kernel may reach another device: no remote copies, remote signals or barrier semaphores. Data moves between devices by JAX's collectives and lax.ppermute only.
A program may use at most 128 MiB of HBM per device.

v0:
```python
import jax
import jax.numpy as jnp
from jax import lax
from jax.sharding import PartitionSpec as P

HD = 128
QH = 16
KVH = 4
QW = 2048
KW = 512


def rms_norm(rows, gain):
    values = rows.astype(jnp.float32)
    scale = lax.rsqrt(jnp.mean(values * values, axis=-1, keepdims=True) + 1e-05)
    return (values * scale * gain.astype(jnp.float32)).astype(jnp.bfloat16)


def rotate(heads, places):
    half = heads.shape[-1] // 2
    freqs = 500000.0 ** (-2.0 * jnp.arange(half, dtype=jnp.float32) / heads.shape[-1])
    angles = places[:, None] * freqs[None, :]
    cosine = jnp.cos(angles)[:, None, :]
    sine = jnp.sin(angles)[:, None, :]
    first = heads[..., :half]
    second = heads[..., half:]
    return jnp.concatenate(
        [first * cosine - second * sine, second * cosine + first * sine], axis=-1
    )


def attend(queries, keys, values, docs):
    length = queries.shape[0]
    local_q = queries.shape[1]
    local_kv = keys.shape[1]
    share = local_q // local_kv
    queries = queries.reshape(length, local_kv, share, HD)
    block = min(512, length)
    scale = 1.0 / HD**0.5
    cols = jnp.arange(length, dtype=jnp.int32)

    def one_block(index):
        start = index * block
        qblock = lax.dynamic_slice_in_dim(queries, start, block, 0)
        scores = (
            jnp.einsum("qkgd,tkd->kgqt", qblock, keys, preferred_element_type=jnp.float32) * scale
        )
        rowpos = start + jnp.arange(block, dtype=jnp.int32)
        rowdoc = lax.dynamic_slice_in_dim(docs, start, block, 0)
        allow = (cols[None, :] <= rowpos[:, None]) & (docs[None, :] == rowdoc[:, None])
        scores = jnp.where(allow[None, None], scores, -1e30)
        peak = jnp.max(scores, axis=-1, keepdims=True)
        expo = jnp.where(allow[None, None], jnp.exp(scores - peak), 0.0)
        total = jnp.sum(expo, axis=-1)
        weights = expo.astype(jnp.bfloat16)
        outs = jnp.einsum("kgqt,tkd->qkgd", weights, values, preferred_element_type=jnp.float32)
        outs = outs / jnp.transpose(total, (2, 0, 1))[..., None]
        return outs.reshape(block, local_q * HD).astype(jnp.bfloat16)

    result = lax.map(one_block, jnp.arange(length // block, dtype=jnp.int32))
    return result.reshape(length, local_q * HD)


def local(tokens, norm_gain, qkv_weight, doc_ids):
    count = lax.axis_size("seq")
    rank = lax.axis_index("seq")
    tok = tokens.shape[1]
    length = tok * count
    local_q = QH // count
    normed = rms_norm(tokens[0], norm_gain)
    all_docs = lax.all_gather(doc_ids, "seq", axis=1, tiled=True)[0]
    proj = jnp.dot(
        normed,
        lax.all_gather(qkv_weight, "dp", axis=0, tiled=True),
        preferred_element_type=jnp.float32,
    )
    places = (rank * tok + jnp.arange(tok, dtype=jnp.int32)).astype(jnp.float32)
    queries = rotate(proj[:, :QW].reshape(tok, QH, HD), places).astype(jnp.bfloat16)
    keys = rotate(proj[:, QW : QW + KW].reshape(tok, KVH, HD), places).astype(jnp.bfloat16)
    values = proj[:, QW + KW :].reshape(tok, KVH, HD).astype(jnp.bfloat16)
    slots = max(KVH, count)
    if slots > KVH:
        keys = jnp.repeat(keys, slots // KVH, axis=1)
        values = jnp.repeat(values, slots // KVH, axis=1)
    q_sent = queries.reshape(tok, count, local_q * HD)
    q_got, k_got, v_got = (
        lax.all_to_all(q_sent, "seq", split_axis=1, concat_axis=0, tiled=True),
        lax.all_to_all(keys, "seq", split_axis=1, concat_axis=0, tiled=True),
        lax.all_to_all(values, "seq", split_axis=1, concat_axis=0, tiled=True),
    )
    q_heads = q_got.reshape(length, local_q, HD)
    outputs = attend(q_heads, k_got, v_got, all_docs)
    back = outputs.reshape(count, tok, local_q * HD)
    return lax.all_to_all(back, "seq", split_axis=0, concat_axis=2, tiled=True)


def solution(mesh):
    in_specs = (P(("group", "dp"), "seq", None), P(), P("dp", None), P(("group", "dp"), "seq"))
    out_specs = P(("group", "dp"), "seq", None)
    return jax.shard_map(local, mesh=mesh, in_specs=in_specs, out_specs=out_specs, check_vma=False)
```

profile of v0, /device:TPU:0, one launch (start us, length us, event | category | flops | bytes accessed | tf_op | source)
XLA Modules:
  0.0 297.0 jit_solution(6609023048014826242)
XLA Ops:
  7.3 0.8 copy-done.1
  9.0 157.5 %all-gather.2.cloned.1.call-done = bf16[4096,3072]{1,0:T(8,128)(2,1)} async-done(((bf16[1024,3072]{1,0:T(8,128)(2,1)}), bf16[4096,3072]{1,0:T(8,128)(2,1)}) %all-gather.2.cloned.1.call-update) | async-done | bytes 25165840 | tf_op jit(solution)/shard_map/all_gather | solution.py:74
  166.4 11.6 %fusion.24 = f32[256,3072]{1,0:T(8,128)S(1)} fusion(bf16[4096,3072]{1,0:T(8,128)(2,1)} %all-gather.2.cloned.1.call-done, bf16[1,256,4096]{2,1,0:T(8,128)(2,1)S(1)} %copy-done.1, f32[4096]{0:T(1024)S(1)} %convert_element_type.47, f32[256]{0:T(256)S(1)} %add_rsqrt_fusion), kind=kOutput, calls=%fused_computation.28 | convolution fusion | flops 6446645248 | bytes 30426112 | tf_op jit(solution)/shard_map/dot_general | solution.py:72
  178.1 1.6 slice.29
  180.4 0.8 copy_bitcast_fusion.2
  181.2 2.0 copy.35
  183.2 4.6 %all-to-all-start.2 = ((bf16[256,4,128]{2,0,1:T(8,128)(2,1)}), bf16[256,4,128]{2,0,1:T(8,128)(2,1)S(1)}, u32[]{:S(2)}, u32[]{:S(2)}) async-start(bf16[256,4,128]{2,0,1:T(8,128)(2,1)} %copy_bitcast_fusion.2), calls=%async_computation.2 | async-start | bytes 524288 | tf_op jit(solution)/shard_map/all_to_all | solution.py:89
  188.1 1.1 pad_maximum_fusion
  189.2 7.9 %all-to-all-done.2 = bf16[256,4,128]{2,0,1:T(8,128)(2,1)S(1)} async-done(((bf16[256,4,128]{2,0,1:T(8,128)(2,1)}), bf16[256,4,128]{2,0,1:T(8,128)(2,1)S(1)}, u32[]{:S(2)}, u32[]{:S(2)}) %all-to-all-start.2) | async-done | bytes 262176 | tf_op jit(solution)/shard_map/all_to_all | solution.py:89
  197.1 3.5 %all-to-all-start = ((bf16[256,4,512]{0,2,1:T(8,128)(2,1)}), bf16[256,4,512]{0,2,1:T(8,128)(2,1)S(1)}, u32[]{:S(2)}, u32[]{:S(2)}) async-start(bf16[256,4,512]{0,2,1:T(8,128)(2,1)} %bitcast.3), calls=%async_computation | async-start | bytes 2097152 | tf_op jit(solution)/shard_map/all_to_all | solution.py:87
  201.5 0.9 pad_maximum_fusion.1
  202.4 22.4 %all-to-all-done = bf16[256,4,512]{0,2,1:T(8,128)(2,1)S(1)} async-done(((bf16[256,4,512]{0,2,1:T(8,128)(2,1)}), bf16[256,4,512]{0,2,1:T(8,128)(2,1)S(1)}, u32[]{:S(2)}, u32[]{:S(2)}) %all-to-all-start) | async-done | bytes 1048608 | tf_op jit(solution)/shard_map/all_to_all | solution.py:87
  224.8 3.4 %all-to-all-start.1 = ((bf16[256,4,128]{2,0,1:T(8,128)(2,1)}), bf16[256,4,128]{2,0,1:T(8,128)(2,1)S(1)}, u32[]{:S(2)}, u32[]{:S(2)}) async-start(bf16[256,4,128]{2,0,1:T(8,128)(2,1)} %pad_maximum_fusion.1), calls=%async_computation.1 | async-start | bytes 524288 | tf_op jit(solution)/shard_map/all_to_all | solution.py:88
  228.2 11.3 %all_gather.6 = s32[1,1024]{1,0:T(1,128)S(1)} all-gather(s32[1,256]{1,0:T(1,128)S(1)} %copy-done.5), channel_id=1, replica_groups=mesh['group'=2,'dp'=4,'seq'=4] {'seq'}, dimensions={1}, use_global_device_ids=true | all-gather | bytes 5120 | tf_op jit(solution)/shard_map/all_gather | solution.py:71
  239.6 1.8 copy.31
  242.2 19.8 %while.11 = (s32[]{:T(128)}, bf16[2,512,512]{2,1,0:T(8,128)(2,1)S(1)}, s32[2]{0:T(128)S(1)}, s32[1,1024]{1,0:T(1,128)S(1)}, s32[1024]{0:T(1024)S(1)}, /*index=5*...) while((s32[]{:T(128)}, ...), condition=%wide.region_4.5_spmd.clone, body=%wide.region_1.4_spmd.clone.sunk | while | flops 1103098368 | bytes 33085660 | solution.py:60
  244.3 1.9 fusion.41
  246.2 2.9 fusion.42
  249.1 2.8 divide_convert_fusion.2
  254.2 1.9 fusion.41
  256.1 2.9 fusion.42
  259.0 2.8 divide_convert_fusion.2
  262.0 26.1 %all_to_all.69 = bf16[4,256,512]{2,1,0:T(8,128)(2,1)S(1)} all-to-all(bf16[4,256,512]{2,1,0:T(8,128)(2,1)S(1)} %bitcast.127), channel_id=1, replica_groups=mesh['group'=2,'dp'=4,'seq'=4] {'seq'}, dimensions={0} | all-to-all | bytes 2097152 | tf_op jit(solution)/shard_map/all_to_all | solution.py:94
  288.7 1.4 copy.34
  (49 shorter events, 8.1 us)
Async XLA Ops:
  6.5 0.7 copy-start.4
  6.5 1.6 copy-start.1
  6.5 159.9 %all-gather.2.cloned.1.call-start = ((), (), s32[]{:S(2)}) async-start(), calls=%async_computation.4 | async-start | bytes 31457280 | tf_op jit(solution)/shard_map/all_gather | solution.py:74
  178.1 2.3 copy-start
  181.2 19.6 %slice-start = ((f32[256,3072]{1,0:T(8,128)}), f32[256,512]{1,0:T(8,128)S(1)}, s32[]{:S(2)}) async-start(f32[256,3072]{1,0:T(8,128)} %copy-done), calls=%async_computation.5 | async-start | bytes 1048576 | tf_op jit(solution)/shard_map/slice | solution.py:79
  183.2 13.9 %all-to-all-start.2 = ((bf16[256,4,128]{2,0,1:T(8,128)(2,1)}), bf16[256,4,128]{2,0,1:T(8,128)(2,1)S(1)}, u32[]{:S(2)}, u32[]{:S(2)}) async-start(bf16[256,4,128]{2,0,1:T(8,128)(2,1)} %copy_bitcast_fusion.2), calls=%async_computation.2 | async-start | bytes 524288 | tf_op jit(solution)/shard_map/all_to_all | solution.py:89
  188.1 40.1 %copy-start.5 = (s32[1,256]{1,0:T(1,128)S(1)}, s32[1,256]{1,0:T(1,128)}, u32[]{:S(2)}) copy-start(s32[1,256]{1,0:T(1,128)} %param.9) | copy-start | bytes 3076
  197.1 27.7 %copy-start.2 = (bf16[256,4,128]{2,0,1:T(8,128)(2,1)}, bf16[256,4,128]{2,0,1:T(8,128)(2,1)S(1)}, u32[]{:S(2)}) copy-start(bf16[256,4,128]{2,0,1:T(8,128)(2,1)S(1)} %all-to-all-done.2) | copy-start | bytes 786436
  197.1 27.7 %all-to-all-start = ((bf16[256,4,512]{0,2,1:T(8,128)(2,1)}), bf16[256,4,512]{0,2,1:T(8,128)(2,1)S(1)}, u32[]{:S(2)}, u32[]{:S(2)}) async-start(bf16[256,4,512]{0,2,1:T(8,128)(2,1)} %bitcast.3), calls=%async_computation | async-start | bytes 2097152 | tf_op jit(solution)/shard_map/all_to_all | solution.py:87
  224.8 17.4 %all-to-all-start.1 = ((bf16[256,4,128]{2,0,1:T(8,128)(2,1)}), bf16[256,4,128]{2,0,1:T(8,128)(2,1)S(1)}, u32[]{:S(2)}, u32[]{:S(2)}) async-start(bf16[256,4,128]{2,0,1:T(8,128)(2,1)} %pad_maximum_fusion.1), calls=%async_computation.1 | async-start | bytes 524288 | tf_op jit(solution)/shard_map/all_to_all | solution.py:88
  246.1 2.9 copy-start.3
  256.1 2.9 copy-start.3
Sparse Core Ops, SparseCore 0:
  8.9 157.4 all-gather.1
where the time goes:
time: 297 us
  waiting for transfers between devices  189 us (64%)
  blocking collectives  37.5 us (13%)
  matrix products  20.9 us (7%)
  between operations  13.6 us (5%)
  local copies, waits for them, and re-layouts  13.5 us (5%)
  starting transfers between devices  11.5 us (4%)
  other arithmetic  10.1 us (3%)
    all_gather x1, waiting for transfers between devices, local(): lax.all_gather(qkv_weight, 'dp', axis=0, tiled=True)  157 us
    all_to_all x1, blocking collectives, local(): return lax.all_to_all(back, 'seq', split_axis=0, concat_axis=2, tiled=True)  26.1 us
    all_to_all x1, waiting for transfers between devices, local(): lax.all_to_all(q_sent, 'seq', split_axis=1, concat_axis=0, tiled=True)  22.4 us
    dot_general x1, matrix products, local(): jnp.dot(normed, lax.all_gather(qkv_weight, 'dp', axis=0, tiled=True), pre...  11.6 us
    all_gather x1, blocking collectives, local(): all_docs = lax.all_gather(doc_ids, 'seq', axis=1, tiled=True)[0]  11.3 us
    all_to_all x1, waiting for transfers between devices, local(): lax.all_to_all(values, 'seq', split_axis=1, concat_axis=0, tiled=True)  7.93 us
  transfers between devices with their start and end apart: 4, of which 3 were waited for; matrix products, arithmetic and copies ran while one was open for 2% of the time, Pallas kernels for 0%

commit v1 on v0

--- a/solution.py
+++ b/solution.py
@@ -8,6 +8,29 @@
 KVH = 4
 QW = 2048
 KW = 512
+
+
+def cut_along(x, dim, devices):
+    dims = x.shape
+    parts = x.reshape(*dims[:dim], devices, dims[dim] // devices, *dims[dim + 1 :])
+    return jnp.moveaxis(parts, dim, 0)
+
+
+def in_order(blocks, dim):
+    blocks = jnp.moveaxis(blocks, 0, dim)
+    lengths = blocks.shape
+    return blocks.reshape(*lengths[:dim], lengths[dim] * lengths[dim + 1], *lengths[dim + 2 :])
+
+
+def swapped_with_each(x, axis, split_dim, concat_dim):
+    size, mine = (lax.axis_size(axis), lax.axis_index(axis))
+    blocks = cut_along(x, split_dim, size)
+    outs = [blocks[mine]]
+    for hop in range(1, size):
+        sent = blocks[mine ^ hop]
+        outs.append(lax.ppermute(sent, axis, [(i, i ^ hop) for i in range(size)]))
+    blocks = jnp.stack(outs)[mine ^ jnp.arange(size)]
+    return in_order(blocks, concat_dim)
 
 
 def rms_norm(rows, gain):
@@ -84,7 +107,7 @@
         values = jnp.repeat(values, slots // KVH, axis=1)
     q_sent = queries.reshape(tok, count, local_q * HD)
     q_got, k_got, v_got = (
-        lax.all_to_all(q_sent, "seq", split_axis=1, concat_axis=0, tiled=True),
+        swapped_with_each(q_sent, "seq", 1, 0),
         lax.all_to_all(keys, "seq", split_axis=1, concat_axis=0, tiled=True),
         lax.all_to_all(values, "seq", split_axis=1, concat_axis=0, tiled=True),
     )

time: 297 us -> 286 us (0.963)
  waiting for transfers between devices: 189 us -> 158 us
  blocking collectives: 37.5 us -> 51.5 us
    all_to_all x1 -> x0, waiting for transfers between devices: 22.4 us -> none  [local(): lax.all_to_all(q_sent, 'seq', split_axis=1, concat_axis=0, tiled=True)]
    all_to_all x1, waiting for transfers between devices: 7.93 us -> 0.01 us  [local(): lax.all_to_all(values, 'seq', split_axis=1, concat_axis=0, tiled=True)]
    all_to_all x1, blocking collectives: 26.1 us -> 33.5 us  [local(): return lax.all_to_all(back, 'seq', split_axis=0, concat_axis=2, tiled=True)]
    all_gather x1, blocking collectives: 11.3 us -> 18 us  [local(): all_docs = lax.all_gather(doc_ids, 'seq', axis=1, tiled=True)[0]]
    ppermute x0 -> x3, starting transfers between devices: none -> 4.53 us  [swapped_with_each(): outs.append(lax.ppermute(sent, axis, [(i, i ^ hop) for i in range(size)]))]
    all_to_all x1 -> x0, starting transfers between devices: 3.52 us -> none  [local(): lax.all_to_all(q_sent, 'seq', split_axis=1, concat_axis=0, tiled=True)]
  transfers between devices with their start and end apart: 4 -> 6, of which waited for: 3 -> 2; matrix products, arithmetic and copies ran while one was open for 2% -> 4% of each run, Pallas kernels for 0% -> 0%
where the time goes in v1:
time: 286 us; the launch traced here: 285 us
  waiting for transfers between devices  158 us (55%)
  blocking collectives  51.5 us (18%)
  matrix products  22.7 us (8%)
  starting transfers between devices  14.2 us (5%)
  between operations  13.6 us (5%)
  local copies, waits for them, and re-layouts  12.3 us (4%)
  other arithmetic  11.8 us (4%)
    all_gather x1, waiting for transfers between devices, local(): lax.all_gather(qkv_weight, 'dp', axis=0, tiled=True)  157 us
    all_to_all x1, blocking collectives, local(): return lax.all_to_all(back, 'seq', split_axis=0, concat_axis=2, tiled=True)  33.5 us
    all_gather x1, blocking collectives, local(): all_docs = lax.all_gather(doc_ids, 'seq', axis=1, tiled=True)[0]  18 us
    dot_general x1, matrix products, local(): jnp.dot(normed, lax.all_gather(qkv_weight, 'dp', axis=0, tiled=True), pre...  11.6 us
    dot_general x2, matrix products, one_block(): jnp.einsum('kgqt,tkd->qkgd', weights, values, preferred_element_type=jnp....  7.38 us
    reduce_sum x2, other arithmetic, one_block(): total = jnp.sum(expo, axis=-1)  5.85 us
  transfers between devices with their start and end apart: 6, of which 2 were waited for; matrix products, arithmetic and copies ran while one was open for 4% of the time, Pallas kernels for 0%

profile of v1, /device:TPU:0, one launch (start us, length us, event | category | flops | bytes accessed | tf_op | source)
XLA Modules:
  0.0 285.3 jit_solution(10566376514191405454)
XLA Ops:
  7.6 0.7 copy.32
  8.4 0.8 copy.34
  9.6 156.8 %all-gather.2.cloned.1.call-done = bf16[4096,3072]{1,0:T(8,128)(2,1)} async-done(((bf16[1024,3072]{1,0:T(8,128)(2,1)}), bf16[4096,3072]{1,0:T(8,128)(2,1)}) %all-gather.2.cloned.1.call-update) | async-done | bytes 25165840 | tf_op jit(solution)/shard_map/all_gather | solution.py:97
  166.4 11.6 %fusion.24 = f32[256,3072]{1,0:T(8,128)S(1)} fusion(bf16[4096,3072]{1,0:T(8,128)(2,1)} %all-gather.2.cloned.1.call-done, bf16[1,256,4096]{2,1,0:T(8,128)(2,1)S(1)} %copy-done, f32[4096]{0:T(1024)S(1)} %convert_element_type.53, f32[256]{0:T(256)S(1)} %add_rsqrt_fusion), kind=kOutput, calls=%fused_computation.29 | convolution fusion | flops 6446645248 | bytes 30426112 | tf_op jit(solution)/shard_map/dot_general | solution.py:95
  178.1 0.7 copy_bitcast_fusion.2
  179.0 4.6 %all-to-all-start.1 = ((bf16[256,4,128]{2,0,1:T(8,128)(2,1)}), bf16[256,4,128]{2,0,1:T(8,128)(2,1)S(1)}, u32[]{:S(2)}, u32[]{:S(2)}) async-start(bf16[256,4,128]{2,0,1:T(8,128)(2,1)} %copy_bitcast_fusion.2), calls=%async_computation.1 | async-start | bytes 524288 | tf_op jit(solution)/shard_map/all_to_all | solution.py:112
  183.6 1.8 copy.41
  185.5 1.9 subtract_convert_fusion
  188.2 2.1 collective-permute-start
  190.3 2.4 collective-permute-start.1
  193.2 0.9 pad_maximum_fusion.1
  194.1 5.0 %all-to-all-start = ((bf16[256,4,128]{2,0,1:T(8,128)(2,1)}), bf16[256,4,128]{2,0,1:T(8,128)(2,1)S(1)}, u32[]{:S(2)}, u32[]{:S(2)}) async-start(bf16[256,4,128]{2,0,1:T(8,128)(2,1)} %pad_maximum_fusion.1), calls=%async_computation | async-start | bytes 524288 | tf_op jit(solution)/shard_map/all_to_all | solution.py:111
  199.1 18.0 %all_gather.6 = s32[1,1024]{1,0:T(1,128)S(1)} all-gather(s32[1,256]{1,0:T(1,128)S(1)} %copy-done.5), channel_id=1, replica_groups=mesh['group'=2,'dp'=4,'seq'=4] {'seq'}, dimensions={1}, use_global_device_ids=true | all-gather | bytes 5120 | tf_op jit(solution)/shard_map/all_gather | solution.py:94
  217.2 1.2 maximum_bitcast_fusion
  219.3 1.8 copy.37
  221.3 21.6 %while.11 = (s32[]{:T(128)}, bf16[2,512,512]{2,1,0:T(8,128)(2,1)S(1)}, s32[2]{0:T(128)S(1)}, s32[1,1024]{1,0:T(1,128)S(1)}, s32[1024]{0:T(1024)S(1)}, /*index=5*...) while((s32[]{:T(128)}, ...), condition=%wide.region_4.5_spmd.clone, body=%wide.region_1.4_spmd.clone.sunk | while | flops 1103098368 | bytes 32037064 | solution.py:83
  223.3 1.9 fusion.42
  225.2 2.9 %fusion.43 = f32[4,512]{1,0:T(4,128)S(1)} fusion(f32[512,4,1024]{2,0,1:T(8,128)S(1)} %get-tuple-element.176, f32[4,512]{1,0:T(4,128)S(1)} %get-tuple-element.177, pred[512,1024]{1,0:T(8,128)(4,1)S(1)} %fusion.41), kind=kLoop, calls=%fused_computation.5.clone.1 | loop fusion | flops 10483712 | bytes 8929280 | tf_op jit(solution)/shard_map/while/body/eval_jaxpr/reduce_sum | solution.py:77
  228.1 3.7 %divide_convert_fusion.2 = bf16[512,1,4,128]{0,3,2,1:T(8,128)(2,1)S(1)} fusion(f32[512,4,1024]{2,0,1:T(8,128)S(1)} %get-tuple-element.176, f32[4,512]{1,0:T(4,128)S(1)} %get-tuple-element.177, pred[512,1024]{1,0:T(8,128)(4,1)S(1)} %fusion.41, f32[512,4]{0,1:T(4,128)S(1)} %bitcast.140, bf16[1024,1,128]{0,2,1:T(8,128)(2,1)} %get-tuple-element.209), kind=kOutput, calls=%fused_computation.13.clone.1 | convolution fusion | flops 547880960 | bytes 9715712 | tf_op jit(solution)/shard_map/while/body/eval_jaxpr/kgqt,tkd->qkgd/dot_general | solution.py:79
  234.1 1.9 fusion.42
  236.0 2.9 %fusion.43 = f32[4,512]{1,0:T(4,128)S(1)} fusion(f32[512,4,1024]{2,0,1:T(8,128)S(1)} %get-tuple-element.176, f32[4,512]{1,0:T(4,128)S(1)} %get-tuple-element.177, pred[512,1024]{1,0:T(8,128)(4,1)S(1)} %fusion.41), kind=kLoop, calls=%fused_computation.5.clone.1 | loop fusion | flops 10483712 | bytes 8929280 | tf_op jit(solution)/shard_map/while/body/eval_jaxpr/reduce_sum | solution.py:77
  238.9 3.7 %divide_convert_fusion.2 = bf16[512,1,4,128]{0,3,2,1:T(8,128)(2,1)S(1)} fusion(f32[512,4,1024]{2,0,1:T(8,128)S(1)} %get-tuple-element.176, f32[4,512]{1,0:T(4,128)S(1)} %get-tuple-element.177, pred[512,1024]{1,0:T(8,128)(4,1)S(1)} %fusion.41, f32[512,4]{0,1:T(4,128)S(1)} %bitcast.140, bf16[1024,1,128]{0,2,1:T(8,128)(2,1)} %get-tuple-element.209), kind=kOutput, calls=%fused_computation.13.clone.1 | convolution fusion | flops 547880960 | bytes 9715712 | tf_op jit(solution)/shard_map/while/body/eval_jaxpr/kgqt,tkd->qkgd/dot_general | solution.py:79
  242.9 33.5 %all_to_all.54 = bf16[4,256,512]{2,1,0:T(8,128)(2,1)S(1)} all-to-all(bf16[4,256,512]{2,1,0:T(8,128)(2,1)S(1)} %bitcast.131), channel_id=1, replica_groups=mesh['group'=2,'dp'=4,'seq'=4] {'seq'}, dimensions={0} | all-to-all | bytes 2097152 | tf_op jit(solution)/shard_map/all_to_all | solution.py:117
  277.0 1.4 copy.40
  (58 shorter events, 8.0 us)
Async XLA Ops:
  6.5 0.7 copy-start.4
  6.5 2.6 copy-start
  6.5 159.9 %all-gather.2.cloned.1.call-start = ((), (), s32[]{:S(2)}) async-start(), calls=%async_computation.3 | async-start | bytes 31457280 | tf_op jit(solution)/shard_map/all_gather | solution.py:97
  179.0 15.1 %all-to-all-start.1 = ((bf16[256,4,128]{2,0,1:T(8,128)(2,1)}), bf16[256,4,128]{2,0,1:T(8,128)(2,1)S(1)}, u32[]{:S(2)}, u32[]{:S(2)}) async-start(bf16[256,4,128]{2,0,1:T(8,128)(2,1)} %copy_bitcast_fusion.2), calls=%async_computation.1 | async-start | bytes 524288 | tf_op jit(solution)/shard_map/all_to_all | solution.py:112
  185.5 7.6 %copy-start.2 = (f32[256,64]{1,0:T(8,128)S(1)}, f32[256,64]{1,0:T(8,128)}, u32[]{:S(2)}) copy-start(f32[256,64]{1,0:T(8,128)} %copy.32) | copy-start | bytes 196612
  185.5 7.6 %copy-start.3 = (f32[256,64]{1,0:T(8,128)S(1)}, f32[256,64]{1,0:T(8,128)}, u32[]{:S(2)}) copy-start(f32[256,64]{1,0:T(8,128)} %copy.34) | copy-start | bytes 196612
  187.4 11.7 %copy-start.5 = (s32[1,256]{1,0:T(1,128)S(1)}, s32[1,256]{1,0:T(1,128)}, u32[]{:S(2)}) copy-start(s32[1,256]{1,0:T(1,128)} %param.9) | copy-start | bytes 3076
  188.2 29.0 %collective-permute-start = (bf16[256,1,512]{2,0,1:T(8,128)(2,1)S(1)}, bf16[256,1,512]{2,0,1:T(8,128)(2,1)S(1)}, u32[]{:S(2)}, u32[]{:S(2)}) collective-permute-start(bf16[256,1,512]{2,0,1:T(8,128)(2,1)S(1)} %bitcast.138), channel_id=1, source_target_pairs={{0,1},{1,0},{2,3},{3,2},{4,5},{5,4},{6,7},{7,6},{8,9},{9,8},{10,11... | collective-permute-start | bytes 786440 | tf_op jit(solution)/shard_map/ppermute | solution.py:31
  190.3 27.0 %collective-permute-start.1 = (bf16[256,1,512]{2,0,1:T(8,128)(2,1)S(1)}, bf16[256,1,512]{2,0,1:T(8,128)(2,1)}, u32[]{:S(2)}, u32[]{:S(2)}) collective-permute-start(bf16[256,1,512]{2,0,1:T(8,128)(2,1)S(1)} %bitcast.137), channel_id=1, source_target_pairs={{0,2},{1,3},{2,0},{3,1},{4,6},{5,7},{6,4},{7,5},{8,10},{9,11},{10,... | collective-permute-start | bytes 786440 | tf_op jit(solution)/shard_map/ppermute | solution.py:31
  192.6 24.6 %collective-permute-start.2 = (bf16[256,1,512]{2,0,1:T(8,128)(2,1)S(1)}, bf16[256,1,512]{2,0,1:T(8,128)(2,1)}, u32[]{:S(2)}, u32[]{:S(2)}) collective-permute-start(bf16[256,1,512]{2,0,1:T(8,128)(2,1)S(1)} %bitcast.136), channel_id=1, source_target_pairs={{0,3},{1,2},{2,1},{3,0},{4,7},{5,6},{6,5},{7,4},{8,11},{9,10},{10,... | collective-permute-start | bytes 786440 | tf_op jit(solution)/shard_map/ppermute | solution.py:31
  194.1 23.2 %copy-start.1 = (bf16[256,4,128]{2,0,1:T(8,128)(2,1)}, bf16[256,4,128]{2,0,1:T(8,128)(2,1)S(1)}, u32[]{:S(2)}) copy-start(bf16[256,4,128]{2,0,1:T(8,128)(2,1)S(1)} %all-to-all-done.1) | copy-start | bytes 786436
  194.1 27.2 %all-to-all-start = ((bf16[256,4,128]{2,0,1:T(8,128)(2,1)}), bf16[256,4,128]{2,0,1:T(8,128)(2,1)S(1)}, u32[]{:S(2)}, u32[]{:S(2)}) async-start(bf16[256,4,128]{2,0,1:T(8,128)(2,1)} %pad_maximum_fusion.1), calls=%async_computation | async-start | bytes 524288 | tf_op jit(solution)/shard_map/all_to_all | solution.py:111
Sparse Core Ops, SparseCore 0:
  8.9 157.4 all-gather.1
